TPU v7x, 32 devices: a whole 2x2x4 slice. The times are simulated.
32 devices in a mesh: section: 8 (over y, x, core), expert: 4 (over z).
Axes of the slice: x: 2, y: 2, z: 4, core: 2. Of those that a mesh axis runs over, the one named last changes fastest.
Arguments:
- acts: bfloat16 [8, 128, 2560], P('section', 'expert'), may hold values from -6 to 6
- incoming: bfloat16 [1, 128, 2560], P(None, 'expert'), may hold values from -6 to 6
- routes: int32 [2, 8, 128, 2], P(None, 'section', 'expert'), may hold values from 0 to 3, all different within a row; in each aligned block of 32 rows (0 to 31, 32 to 63, ..., all dimensions but the last counted through in order) at most 24 rows name the same one
- route_weight: float32 [2, 8, 128, 2], P(None, 'section', 'expert'), may hold values from 0.25 to 1
- norm_gain: float32 [8, 2560], P('section'), may hold values from 0.25 to 1.75
- w_gate: bfloat16 [8, 2560, 3072], P('section', None, 'expert'), may hold values from -0.125 to 0.125
- w_up: bfloat16 [8, 2560, 3072], P('section', None, 'expert'), may hold values from -0.125 to 0.125
- w_down: bfloat16 [8, 3072, 2560], P('section', 'expert'), may hold values from -0.21875 to 0.21875
Outputs:
- section_outputs: bfloat16 [2, 8, 128, 2560], P(None, 'section', 'expert')
Inputs may be any that keep to these rules, and one draw needn't show every extreme that they name: `routes`: a token's 2 experts are distinct; in each aligned block of 32 tokens (the tokens of one device) no expert is chosen more than 24 times, and that count is reached.
All inputs are finite; a program needn't handle non-finite values.
Results may differ from a plain program's by a relative error of at most 0.009.
Values may be sent and summed in bfloat16 or wider, within the bound.
A program may use at most 64 MiB of HBM per device.

v0:
```python
import jax
import jax.numpy as jnp
from jax import lax
from jax.sharding import PartitionSpec as P

EXPERTS = 4
TICKS = 2
CAP = 24


def shifted(block, axis, distance):
    devices = range(lax.axis_size(axis))
    route = [(i - distance, i) for i in devices if i - distance in devices]
    return lax.ppermute(block, axis, route)


def norm_rows(tokens_in, gain):
    tok_f = tokens_in.astype(jnp.float32)
    return (
        tok_f * lax.rsqrt(jnp.mean(tok_f * tok_f, axis=-1, keepdims=True) + 1e-06) * gain
    ).astype(jnp.bfloat16)


def slot_tables(chosen):
    expert_hot = (chosen[:, :, None] == jnp.arange(EXPERTS, dtype=jnp.int32)[None, None, :]).astype(
        jnp.int32
    )
    flat_hot = expert_hot.reshape(-1, EXPERTS)
    before = jnp.cumsum(flat_hot, axis=0) - flat_hot
    slot_num = jnp.sum(before * flat_hot, axis=-1).reshape(chosen.shape)
    slot_hot = (slot_num[:, :, None] == jnp.arange(CAP, dtype=jnp.int32)[None, None, :]).astype(
        jnp.float32
    )
    return (expert_hot.astype(jnp.float32), slot_hot)


def expert_rows(arrived, w_gate, w_up, w_down):
    flat_rows = arrived.reshape(-1, arrived.shape[-1])
    gate_val = jnp.dot(flat_rows, w_gate, preferred_element_type=jnp.float32)
    up_val = jnp.dot(flat_rows, w_up, preferred_element_type=jnp.float32)
    hidden = (jax.nn.silu(gate_val) * up_val).astype(jnp.bfloat16)
    partial_value = jnp.dot(hidden, w_down, preferred_element_type=jnp.float32).astype(jnp.bfloat16)
    return partial_value.reshape(arrived.shape)


def send_back(partial_value):
    return lax.all_to_all(partial_value, "expert", split_axis=0, concat_axis=0, tiled=True)


def section_layer(tokens_in, chosen, chosen_weight, gain, w_gate, w_up, w_down):
    tok_count = tokens_in.shape[0]
    width = tokens_in.shape[1]
    devices = lax.axis_size("expert")
    group = devices // EXPERTS
    normed = norm_rows(tokens_in, gain)
    expert_hot, slot_hot = slot_tables(chosen)
    picker = jnp.einsum("tke,tkc->ect", expert_hot, slot_hot).astype(jnp.bfloat16)
    picked = jnp.dot(
        picker.reshape(EXPERTS * CAP, tok_count), normed, preferred_element_type=jnp.float32
    )
    picked = picked.astype(jnp.bfloat16).reshape(EXPERTS, CAP, width)
    outgoing = jnp.repeat(picked, group, axis=0)
    returned = send_back(
        expert_rows(
            lax.all_to_all(outgoing, "expert", split_axis=0, concat_axis=0, tiled=True),
            w_gate,
            w_up,
            w_down,
        )
    )
    summed = (
        returned.astype(jnp.float32)
        .reshape(EXPERTS, group, CAP, width)
        .sum(axis=1)
        .reshape(EXPERTS * CAP, width)
    )
    mixing = jnp.einsum("tk,tke,tkc->tec", chosen_weight, expert_hot, slot_hot).reshape(
        tok_count, EXPERTS * CAP
    )
    routed = jnp.dot(mixing, summed, precision=lax.Precision.HIGHEST)
    return (tokens_in.astype(jnp.float32) + routed).astype(jnp.bfloat16)


def shards(acts, incoming, routes, route_weight, norm_gain, w_gate, w_up, w_down):
    state = acts[0]
    results = []
    first_section = lax.axis_index("section") == 0
    for tick in range(TICKS):
        layer_out = section_layer(
            state,
            routes[tick, 0],
            route_weight[tick, 0],
            norm_gain[0],
            w_gate[0],
            w_up[0],
            w_down[0],
        )
        results.append(layer_out)
        if tick + 1 < TICKS:
            moved = shifted(layer_out, "section", 1)
            state = jnp.where(first_section, incoming[tick], moved)
    return jnp.stack(results)[:, None]


def solution(mesh):
    placed = (
        P("section", "expert", None),
        P(None, "expert", None),
        P(None, "section", "expert", None),
        P(None, "section", "expert", None),
        P("section", None),
        P("section", None, "expert"),
        P("section", None, "expert"),
        P("section", "expert", None),
    )
    return jax.shard_map(
        shards,
        mesh=mesh,
        in_specs=placed,
        out_specs=P(None, "section", "expert", None),
        check_vma=False,
    )
```

profile of v0, /device:TPU:0, one launch (start us, length us, event | category | flops | bytes accessed | tf_op | source)
XLA Modules:
  0.0 99.8 jit_solution(9765792961046344814)
XLA Ops:
  0.0 0.7 slice_bitcast_fusion.3
  1.5 0.4 fusion.35
  1.9 1.1 %fusion.42 = f32[32]{0:T(128)S(1)} fusion(bf16[1,32,2560]{2,1,0:T(8,128)(2,1)} %param.8), kind=kLoop, calls=%fused_computation.36 | loop fusion | flops 245728 | bytes 163968 | tf_op jit(solution)/shard_map/reduce_sum | solution.py:20
  3.0 0.7 reduce
  3.7 2.0 %convolution_convert_fusion.1 = bf16[96,2560]{1,0:T(8,128)(2,1)} fusion(bf16[96,32]{0,1:T(8,128)(2,1)S(1)} %reshape.72, bf16[1,32,2560]{2,1,0:T(8,128)(2,1)} %param.8, f32[2560]{0:T(1024)S(1)} %reduce, f32[32]{0:T(128)S(1)} %add_rsqrt_fusion.1), kind=kOutput, calls=%fused_computation.15 | convolution fusion | flops 16302080 | bytes 671872 | tf_op jit(solution)/shard_map/dot_general | solution.py:58
  5.8 6.3 %all-to-all-start = ((bf16[4,24,2560]{2,1,0:T(8,128)(2,1)}), bf16[4,24,2560]{2,1,0:T(8,128)(2,1)S(1)}, u32[]{:S(2)}, u32[]{:S(2)}) async-start(bf16[4,24,2560]{2,1,0:T(8,128)(2,1)} %bitcast.5), calls=%async_computation | async-start | bytes 983040 | tf_op jit(solution)/shard_map/all_to_all | solution.py:65
  12.1 13.8 %all-to-all-done = bf16[4,24,2560]{2,1,0:T(8,128)(2,1)S(1)} async-done(((bf16[4,24,2560]{2,1,0:T(8,128)(2,1)}), bf16[4,24,2560]{2,1,0:T(8,128)(2,1)S(1)}, u32[]{:S(2)}, u32[]{:S(2)}) %all-to-all-start) | async-done | bytes 491552 | tf_op jit(solution)/shard_map/all_to_all | solution.py:65
  25.9 2.9 %fusion.10 = f32[96,768]{1,0:T(8,128)S(1)} fusion(bf16[96,2560]{1,0:T(8,128)(2,1)S(1)} %bitcast.100, bf16[1,2560,768]{2,1,0:T(8,128)(2,1)} %param.13), kind=kOutput, calls=%fused_computation.10 | convolution fusion | flops 377487360 | bytes 4718592 | tf_op jit(solution)/shard_map/dot_general | solution.py:39
  28.8 5.8 %fusion.12 = bf16[96,2560]{1,0:T(8,128)(2,1)} fusion(bf16[1,768,2560]{2,1,0:T(8,128)(2,1)} %param.15, bf16[96,2560]{1,0:T(8,128)(2,1)S(1)} %bitcast.101, bf16[1,2560,768]{2,1,0:T(8,128)(2,1)} %param.14, f32[96,768]{1,0:T(8,128)S(1)} %fusion.10), kind=kOutput, calls=%fused_computation.12 | convolution fusion | flops 755662848 | bytes 9142272 | tf_op jit(solution)/shard_map/dot_general | solution.py:42
  34.6 3.5 %all-to-all-start.1 = ((bf16[4,24,2560]{2,1,0:T(8,128)(2,1)}), bf16[4,24,2560]{2,1,0:T(8,128)(2,1)S(1)}, u32[]{:S(2)}, u32[]{:S(2)}) async-start(bf16[4,24,2560]{2,1,0:T(8,128)(2,1)} %bitcast.10), calls=%async_computation.1 | async-start | bytes 983040 | tf_op jit(solution)/shard_map/all_to_all | solution.py:47
  39.0 0.4 fusion.76
  39.4 12.0 %all-to-all-done.1 = bf16[4,24,2560]{2,1,0:T(8,128)(2,1)S(1)} async-done(((bf16[4,24,2560]{2,1,0:T(8,128)(2,1)}), bf16[4,24,2560]{2,1,0:T(8,128)(2,1)S(1)}, u32[]{:S(2)}, u32[]{:S(2)}) %all-to-all-start.1) | async-done | bytes 491552 | tf_op jit(solution)/shard_map/all_to_all | solution.py:47
  51.4 0.6 fusion.21
  52.0 1.3 %collective-permute-start = (bf16[32,2560]{1,0:T(8,128)(2,1)S(1)}, bf16[32,2560]{1,0:T(8,128)(2,1)S(1)}, u32[]{:S(2)}, u32[]{:S(2)}) collective-permute-start(bf16[32,2560]{1,0:T(8,128)(2,1)S(1)} %fusion.21), channel_id=1, source_target_pairs={{0,4},{4,8},{8,12},{12,16},{16,20},{20,24},{24,28},{1,5},{5,9},{9,... | collective-permute-start | bytes 491528 | tf_op jit(solution)/shard_map/ppermute | solution.py:14
  53.3 0.4 fusion.36
  53.8 0.5 collective-permute-done
  54.9 16.4 %all_to_all.20 = bf16[4,24,2560]{2,1,0:T(8,128)(2,1)S(1)} all-to-all(bf16[4,24,2560]{2,1,0:T(8,128)(2,1)S(1)} %bitcast.104), channel_id=1, replica_groups=mesh['section'=8,'expert'=4] {'expert'}, dimensions={0} | all-to-all | bytes 983040 | tf_op jit(solution)/shard_map/all_to_all | solution.py:65
  71.3 2.9 %fusion.8 = f32[96,768]{1,0:T(8,128)S(1)} fusion(bf16[96,2560]{1,0:T(8,128)(2,1)S(1)} %bitcast.102, bf16[1,2560,768]{2,1,0:T(8,128)(2,1)} %param.13), kind=kOutput, calls=%fused_computation.8 | convolution fusion | flops 377487360 | bytes 4718592 | tf_op jit(solution)/shard_map/dot_general | solution.py:39
  74.2 5.8 %fusion.15 = bf16[96,2560]{1,0:T(8,128)(2,1)} fusion(bf16[1,768,2560]{2,1,0:T(8,128)(2,1)} %param.15, bf16[96,2560]{1,0:T(8,128)(2,1)S(1)} %bitcast.103, bf16[1,2560,768]{2,1,0:T(8,128)(2,1)} %param.14, f32[96,768]{1,0:T(8,128)S(1)} %fusion.8), kind=kOutput, calls=%fused_computation.13 | convolution fusion | flops 755662848 | bytes 9142272 | tf_op jit(solution)/shard_map/dot_general | solution.py:42
  80.0 3.5 %all-to-all-start.3 = ((bf16[4,24,2560]{2,1,0:T(8,128)(2,1)}), bf16[4,24,2560]{2,1,0:T(8,128)(2,1)S(1)}, u32[]{:S(2)}, u32[]{:S(2)}) async-start(bf16[4,24,2560]{2,1,0:T(8,128)(2,1)} %bitcast.19), calls=%async_computation.3 | async-start | bytes 983040 | tf_op jit(solution)/shard_map/all_to_all | solution.py:47
  83.5 0.4 fusion.71
  84.0 14.5 %all-to-all-done.3 = bf16[4,24,2560]{2,1,0:T(8,128)(2,1)S(1)} async-done(((bf16[4,24,2560]{2,1,0:T(8,128)(2,1)}), bf16[4,24,2560]{2,1,0:T(8,128)(2,1)S(1)}, u32[]{:S(2)}, u32[]{:S(2)}) %all-to-all-start.3) | async-done | bytes 491552 | tf_op jit(solution)/shard_map/all_to_all | solution.py:47
  98.4 0.6 fusion.22
  99.0 0.8 maximum_bitcast_fusion
  (29 shorter events, 2.4 us)
Async XLA Ops:
  5.8 20.1 %all-to-all-start = ((bf16[4,24,2560]{2,1,0:T(8,128)(2,1)}), bf16[4,24,2560]{2,1,0:T(8,128)(2,1)S(1)}, u32[]{:S(2)}, u32[]{:S(2)}) async-start(bf16[4,24,2560]{2,1,0:T(8,128)(2,1)} %bitcast.5), calls=%async_computation | async-start | bytes 983040 | tf_op jit(solution)/shard_map/all_to_all | solution.py:65
  28.8 9.3 %copy-start.2 = (f32[2,1,32,2]{2,3,1,0:T(2,128)S(1)}, f32[2,1,32,2]{2,3,1,0:T(2,128)}, u32[]{:S(2)}) copy-start(f32[2,1,32,2]{2,3,1,0:T(2,128)} %param.11) | copy-start | bytes 1540
  28.8 22.6 %copy-start = (bf16[1,32,2560]{2,1,0:T(8,128)(2,1)S(1)}, bf16[1,32,2560]{2,1,0:T(8,128)(2,1)}, u32[]{:S(2)}) copy-start(bf16[1,32,2560]{2,1,0:T(8,128)(2,1)} %param.8) | copy-start | bytes 491524
  28.8 25.6 %copy-start.1 = (bf16[1,32,2560]{2,1,0:T(8,128)(2,1)S(1)}, bf16[1,32,2560]{2,1,0:T(8,128)(2,1)}, u32[]{:S(2)}) copy-start(bf16[1,32,2560]{2,1,0:T(8,128)(2,1)} %param.9) | copy-start | bytes 491524
  34.6 16.8 %all-to-all-start.1 = ((bf16[4,24,2560]{2,1,0:T(8,128)(2,1)}), bf16[4,24,2560]{2,1,0:T(8,128)(2,1)S(1)}, u32[]{:S(2)}, u32[]{:S(2)}) async-start(bf16[4,24,2560]{2,1,0:T(8,128)(2,1)} %bitcast.10), calls=%async_computation.1 | async-start | bytes 983040 | tf_op jit(solution)/shard_map/all_to_all | solution.py:47
  52.0 2.3 %collective-permute-start = (bf16[32,2560]{1,0:T(8,128)(2,1)S(1)}, bf16[32,2560]{1,0:T(8,128)(2,1)S(1)}, u32[]{:S(2)}, u32[]{:S(2)}) collective-permute-start(bf16[32,2560]{1,0:T(8,128)(2,1)S(1)} %fusion.21), channel_id=1, source_target_pairs={{0,4},{4,8},{8,12},{12,16},{16,20},{20,24},{24,28},{1,5},{5,9},{9,... | collective-permute-start | bytes 491528 | tf_op jit(solution)/shard_map/ppermute | solution.py:14
  80.0 18.5 %all-to-all-start.3 = ((bf16[4,24,2560]{2,1,0:T(8,128)(2,1)}), bf16[4,24,2560]{2,1,0:T(8,128)(2,1)S(1)}, u32[]{:S(2)}, u32[]{:S(2)}) async-start(bf16[4,24,2560]{2,1,0:T(8,128)(2,1)} %bitcast.19), calls=%async_computation.3 | async-start | bytes 983040 | tf_op jit(solution)/shard_map/all_to_all | solution.py:47
where the time goes:
time: 101 us; the launch traced here: 99.8 us
  waiting for transfers between devices  40.8 us (40%)
  matrix products  22.5 us (22%)
  blocking collectives  16.4 us (16%)
  starting transfers between devices  14.6 us (14%)
  other arithmetic  3.45 us (3%)
  local copies, waits for them, and re-layouts  1.85 us (2%)
    all_to_all x2, waiting for transfers between devices, send_back(): lax.all_to_all(partial_value, 'expert', split_axis=0, concat_axis=0, tile...  26.5 us
    all_to_all x1, blocking collectives, section_layer(): lax.all_to_all(outgoing, 'expert', split_axis=0, concat_axis=0, tiled=True)  16.4 us
    all_to_all x1, waiting for transfers between devices, section_layer(): lax.all_to_all(outgoing, 'expert', split_axis=0, concat_axis=0, tiled=True)  13.8 us
    dot_general x2, matrix products, expert_rows(): jnp.dot(hidden, w_down, preferred_element_type=jnp.float32)  11.6 us
    all_to_all x2, starting transfers between devices, send_back(): lax.all_to_all(partial_value, 'expert', split_axis=0, concat_axis=0, tile...  6.93 us
    all_to_all x1, starting transfers between devices, section_layer(): lax.all_to_all(outgoing, 'expert', split_axis=0, concat_axis=0, tiled=True)  6.35 us
    dot_general x2, matrix products, expert_rows(): gate_val = jnp.dot(flat_rows, w_gate, preferred_element_type=jnp.float32)  5.73 us
    dot_general x2, matrix products, section_layer(): jnp.dot(picker.reshape(EXPERTS * CAP, tok_count), normed, preferred_eleme...  2.36 us
  transfers between devices with their start and end apart: 4, of which 4 were waited for; matrix products, arithmetic and copies ran while one was open for 2% of the time, Pallas kernels for 0%

commit v1 on v0

v1 whole, which is shorter than its diff:
```python
import functools

import jax
import jax.numpy as jnp
from jax import lax
from jax.experimental import pallas as pl
from jax.experimental.pallas import tpu as pltpu
from jax.sharding import PartitionSpec as P

MESH = pl.DeviceIdType.MESH
EXPERTS = 4
CHUNKS = 2
RIGHT, LEFT = 0, 1


def kernel(
    n,
    sections,
    acts,
    incoming,
    routes,
    route_weight,
    gain,
    w_gate_hbm,
    w_up_hbm,
    w_down_hbm,
    out,
    w_gate,
    w_up,
    w_down,
    xbuf,
    mixbuf,
    rsin,
    rsout,
    held,
    moved,
    w_sem,
    own_sem,
    inc_sem,
    ag_send,
    ag_recv,
    mix_send,
    mix_recv,
    rs_send,
    rs_recv,
    move_send,
    move_recv,
):
    s = lax.axis_index("section")
    e = lax.axis_index("expert")
    ticks, _, chunks, tokens, cols = xbuf.shape
    group = n // EXPERTS
    width = chunks * cols
    has_right = e < n - 1
    has_left = e > 0
    has_next = s < sections - 1
    has_prev = s > 0
    right = (s, jnp.minimum(e + 1, n - 1))
    left = (s, jnp.maximum(e - 1, 0))
    following = (jnp.minimum(s + 1, sections - 1), e)
    previous = (jnp.maximum(s - 1, 0), e)
    has = (has_right, has_left)
    peer = (right, left)

    weight_copies = [
        pltpu.make_async_copy(src, dst, w_sem.at[i])
        for i, (src, dst) in enumerate(
            ((w_gate_hbm, w_gate), (w_up_hbm, w_up), (w_down_hbm, w_down))
        )
    ]

    def own_copy(c):
        return pltpu.make_async_copy(
            acts.at[:, pl.ds(c * cols, cols)], xbuf.at[0, e, c], own_sem.at[c]
        )

    def inc_copy(t, c):
        return pltpu.make_async_copy(
            incoming.at[t - 1, :, pl.ds(c * cols, cols)], xbuf.at[t, e, c], inc_sem.at[t, c]
        )

    def ag_copy(way, t, j, c):
        return pltpu.make_async_remote_copy(
            xbuf.at[t, j, c],
            xbuf.at[t, j, c],
            ag_send.at[way, t, j, c],
            ag_recv.at[way, t, j, c],
            device_id=peer[way],
            device_id_type=MESH,
        )

    def mix_copy(way, j):
        return pltpu.make_async_remote_copy(
            mixbuf.at[j],
            mixbuf.at[j],
            mix_send.at[way, j],
            mix_recv.at[way, j],
            device_id=peer[way],
            device_id_type=MESH,
        )

    def rs_copy(way, t, j, c):
        return pltpu.make_async_remote_copy(
            rsout.at[t, j, c],
            rsin.at[way, t, j, c],
            rs_send.at[way, t, j, c],
            rs_recv.at[way, t, j, c],
            device_id=peer[way],
            device_id_type=MESH,
        )

    def move_copy(t, c):
        return pltpu.make_async_remote_copy(
            moved.at[t, c],
            xbuf.at[t + 1, e, c],
            move_send.at[t, c],
            move_recv.at[t, c],
            device_id=following,
            device_id_type=MESH,
        )

    for c in range(chunks):
        own_copy(c).start()

    barrier = pltpu.get_barrier_semaphore()
    around = (
        (has_right, right),
        (has_left, left),
        (has_next, following),
        (has_prev, previous),
    )
    for there, device in around:

        @pl.when(there)
        def _():
            pl.semaphore_signal(barrier, inc=1, device_id=device, device_id_type=MESH)

    for copy in weight_copies:
        copy.start()

    @pl.when(jnp.logical_not(has_prev))
    def _():
        for t in range(1, ticks):
            for c in range(chunks):
                inc_copy(t, c).start()

    rows = ticks * tokens
    lanes = mixbuf.shape[2]
    eye = lax.broadcasted_iota(jnp.int32, (rows, lanes), 0) == lax.broadcasted_iota(
        jnp.int32, (rows, lanes), 1
    )
    chosen = routes[...]
    chosen_weight = route_weight[...]
    mixbuf[e] = jnp.zeros_like(mixbuf[e])
    for x in range(EXPERTS):
        column = jnp.sum(jnp.where(chosen == x, chosen_weight, 0.0), axis=1, keepdims=True)
        mixbuf[e, x : x + 1, :] = jnp.sum(
            jnp.where(eye, column, 0.0), axis=0, keepdims=True
        )

    pl.semaphore_wait(barrier, sum(jnp.where(there, 1, 0) for there, _ in around))

    def send_own(t, c):
        for way in (RIGHT, LEFT):

            @pl.when(has[way])
            def _():
                ag_copy(way, t, e, c).start()

    def partial_of(t, j):
        squares = jnp.zeros((tokens, 1), jnp.float32)
        for c in range(chunks):
            piece = xbuf[t, j, c].astype(jnp.float32)
            squares = squares + jnp.sum(piece * piece, axis=1, keepdims=True)
        scale = lax.rsqrt(squares * (1.0 / width) + 1e-06)
        gate_val = up_val = None
        for c in range(chunks):
            span = pl.ds(c * cols, cols)
            normed = (xbuf[t, j, c].astype(jnp.float32) * scale * gain[:, span]).astype(
                jnp.bfloat16
            )
            gate_part = jnp.dot(normed, w_gate[span, :], preferred_element_type=jnp.float32)
            up_part = jnp.dot(normed, w_up[span, :], preferred_element_type=jnp.float32)
            gate_val = gate_part if gate_val is None else gate_val + gate_part
            up_val = up_part if up_val is None else up_val + up_part
        hidden = (jax.nn.silu(gate_val) * up_val).astype(jnp.bfloat16)
        expert = e // group
        row = mixbuf[j, pl.ds(expert, 1), :]
        pick = (
            lax.broadcasted_iota(jnp.int32, (tokens, lanes), 0) + t * tokens
            == lax.broadcasted_iota(jnp.int32, (tokens, lanes), 1)
        )
        mixing = jnp.sum(jnp.where(pick, row, 0.0), axis=1, keepdims=True)
        for c in range(chunks):
            span = pl.ds(c * cols, cols)
            value = jnp.dot(hidden, w_down[:, span], preferred_element_type=jnp.float32) * mixing
            held[j, c] = value
            for way, first in (
                (RIGHT, jnp.logical_and(jnp.logical_not(has_left), j > e)),
                (LEFT, jnp.logical_and(jnp.logical_not(has_right), j < e)),
            ):

                @pl.when(first)
                def _():
                    rsout[t, j, c] = value.astype(jnp.bfloat16)
                    rs_copy(way, t, j, c).start()

    def tick(t, _):
        for c in range(chunks):

            @pl.when(t == 0)
            def _():
                own_copy(c).wait()

            @pl.when(jnp.logical_and(t > 0, has_prev))
            def _():
                move_copy(jnp.maximum(t - 1, 0), c).wait_recv()

            @pl.when(jnp.logical_and(t > 0, jnp.logical_not(has_prev)))
            def _():
                inc_copy(jnp.maximum(t, 1), c).wait()

            send_own(t, c)

        @pl.when(t == 0)
        def _():
            for way in (RIGHT, LEFT):

                @pl.when(has[way])
                def _():
                    mix_copy(way, e).start()

            for copy in weight_copies:
                copy.wait()

        def arrive(k, _):
            for c in range(chunks):
                for way, j in ((RIGHT, e - k), (LEFT, e + k)):

                    @pl.when(jnp.logical_and(k > 0, jnp.logical_and(j >= 0, j < n)))
                    def _():
                        ag_copy(way, t, j, c).wait_recv()

                        @pl.when(has[way])
                        def _():
                            ag_copy(way, t, j, c).start()

                        if c == 0:

                            @pl.when(t == 0)
                            def _():
                                mix_copy(way, j).wait_recv()

                                @pl.when(has[way])
                                def _():
                                    mix_copy(way, j).start()

            def side(way, _):
                j = e + k * (2 * way - 1)

                @pl.when(
                    jnp.logical_and(
                        jnp.logical_and(j >= 0, j < n), jnp.logical_or(k > 0, way == 0)
                    )
                )
                def _():
                    partial_of(t, j)

                return 0

            return lax.fori_loop(0, 2, side, 0)

        lax.fori_loop(0, n, arrive, 0)

        from_right, from_left = 2 * (n - 1 - e), 2 * e
        last = jnp.maximum(from_right, from_left)

        def combine(time, _):
            for c in range(chunks):
                for way, there, k, j in (
                    (LEFT, has_right, time - from_right, e - (time - from_right)),
                    (RIGHT, has_left, time - from_left, e + (time - from_left)),
                ):

                    @pl.when(
                        jnp.logical_and(
                            there, jnp.logical_and(k >= 0, jnp.logical_and(j >= 0, j < n))
                        )
                    )
                    def _():
                        rs_copy(way, t, j, c).wait_recv()
                        total = held[j, c] + rsin[way, t, j, c].astype(jnp.float32)

                        @pl.when(k == 0)
                        def _():
                            held[j, c] = total

                        @pl.when(k > 0)
                        def _():
                            rsout[t, j, c] = total.astype(jnp.bfloat16)
                            rs_copy(way, t, j, c).start()

                @pl.when(time == last)
                def _():
                    layer = (xbuf[t, e, c].astype(jnp.float32) + held[e, c]).astype(jnp.bfloat16)
                    out[t, :, pl.ds(c * cols, cols)] = layer

                    @pl.when(jnp.logical_and(t < ticks - 1, has_next))
                    def _():
                        moved[jnp.minimum(t, ticks - 2), c] = layer
                        move_copy(jnp.minimum(t, ticks - 2), c).start()

            return 0

        lax.fori_loop(0, 3 * (n - 1) + 1, combine, 0)
        return 0

    lax.fori_loop(0, ticks, tick, 0)

    def drain(j, _):
        for way, within in (
            (RIGHT, jnp.logical_and(has_right, j <= e)),
            (LEFT, jnp.logical_and(has_left, j >= e)),
        ):

            @pl.when(within)
            def _():
                mix_copy(way, j).wait_send()
                for t in range(ticks):
                    for c in range(chunks):
                        ag_copy(way, t, j, c).wait_send()

        for way, within in ((RIGHT, j > e), (LEFT, j < e)):

            @pl.when(within)
            def _():
                for t in range(ticks):
                    for c in range(chunks):
                        rs_copy(way, t, j, c).wait_send()

        return 0

    lax.fori_loop(0, n, drain, 0)

    @pl.when(has_next)
    def _():
        for t in range(ticks - 1):
            for c in range(chunks):
                move_copy(t, c).wait_send()


def solution(mesh):
    n = mesh.shape["expert"]
    sections = mesh.shape["section"]

    def shards(acts, incoming, routes, route_weight, norm_gain, w_gate, w_up, w_down):
        ticks, _, tokens, top = routes.shape
        width, hidden = w_gate.shape[1:]
        chunks = CHUNKS
        cols = width // chunks
        lanes = -(-ticks * tokens // 128) * 128
        half = jnp.bfloat16
        anywhere = pl.BlockSpec(memory_space=pl.ANY)
        vmem = pl.BlockSpec(memory_space=pltpu.VMEM)
        dma = pltpu.SemaphoreType.DMA
        result = pl.pallas_call(
            functools.partial(kernel, n, sections),
            out_shape=jax.ShapeDtypeStruct((ticks, tokens, width), half),
            in_specs=[anywhere, anywhere, vmem, vmem, vmem, anywhere, anywhere, anywhere],
            out_specs=vmem,
            scratch_shapes=[
                pltpu.VMEM((width, hidden), half),
                pltpu.VMEM((width, hidden), half),
                pltpu.VMEM((hidden, width), half),
                pltpu.VMEM((ticks, n, chunks, tokens, cols), half),
                pltpu.VMEM((n, 8, lanes), jnp.float32),
                pltpu.VMEM((2, ticks, n, chunks, tokens, cols), half),
                pltpu.VMEM((ticks, n, chunks, tokens, cols), half),
                pltpu.VMEM((n, chunks, tokens, cols), jnp.float32),
                pltpu.VMEM((ticks - 1, chunks, tokens, cols), half),
                dma((3,)),
                dma((chunks,)),
                dma((ticks, chunks)),
                dma((2, ticks, n, chunks)),
                dma((2, ticks, n, chunks)),
                dma((2, n)),
                dma((2, n)),
                dma((2, ticks, n, chunks)),
                dma((2, ticks, n, chunks)),
                dma((ticks - 1, chunks)),
                dma((ticks - 1, chunks)),
            ],
            compiler_params=pltpu.CompilerParams(
                collective_id=0, has_side_effects=True, vmem_limit_bytes=56 << 20
            ),
        )(
            acts[0],
            incoming,
            routes.reshape(ticks * tokens, top),
            route_weight.reshape(ticks * tokens, top),
            norm_gain,
            w_gate[0],
            w_up[0],
            w_down[0],
        )
        return result[:, None]

    return jax.shard_map(
        shards,
        mesh=mesh,
        in_specs=(
            P("section", "expert", None),
            P(None, "expert", None),
            P(None, "section", "expert", None),
            P(None, "section", "expert", None),
            P("section", None),
            P("section", None, "expert"),
            P("section", None, "expert"),
            P("section", "expert", None),
        ),
        out_specs=P(None, "section", "expert", None),
        check_vma=False,
    )
```

time: 101 us -> 70.2 us (0.70)
  Pallas kernels: 0 us -> 65.5 us
  waiting for transfers between devices: 40.8 us -> 0 us
  matrix products: 22.5 us -> 0 us
  blocking collectives: 16.4 us -> 0 us
  starting transfers between devices: 14.6 us -> 0 us
  other arithmetic: 3.45 us -> 0 us
  local copies, waits for them, and re-layouts: 1.85 us -> 4.48 us
    pallas_call x0 -> x1, Pallas kernels: none -> 65.5 us  [shards(): pl.pallas_call(functools.partial(kernel, n, sections), out_shape=jax.Shap...]
    all_to_all x3 -> x0, waiting for transfers between devices: 40.3 us -> none  [the longest x2 26.5 us: send_back(): lax.all_to_all(partial_value, 'expert', split_axis=0, concat_axis=0, tile...]
    dot_general x12 -> x0, matrix products: 22.5 us -> none  [the longest x2 11.6 us: expert_rows(): jnp.dot(hidden, w_down, preferred_element_type=jnp.float32)]
    all_to_all x1 -> x0, blocking collectives: 16.4 us -> none  [section_layer(): lax.all_to_all(outgoing, 'expert', split_axis=0, concat_axis=0, tiled=True)]
    all_to_all x3 -> x0, starting transfers between devices: 13.3 us -> none  [the longest x2 6.93 us: send_back(): lax.all_to_all(partial_value, 'expert', split_axis=0, concat_axis=0, tile...]
    reshape x2, local copies, waits for them, and re-layouts: 0.19 us -> 2.76 us  [the longest x1 1.38 us: shards(): routes.reshape(ticks * tokens, top)]
    unnamed x6 -> x1, local copies, waits for them, and re-layouts: 0.02 us -> 1.72 us
    reduce_sum x4 -> x0, other arithmetic: 1.59 us -> none  [the longest x2 1.23 us: norm_rows(): jnp.mean(tok_f * tok_f, axis=-1, keepdims=True) + 1e-06]
  transfers between devices with their start and end apart: 4 -> 0, of which waited for: 4 -> 0; matrix products, arithmetic and copies ran while one was open for 2% -> 0% of each run, Pallas kernels for 0% -> 0%
where the time goes in v1:
time: 70.2 us; the launch traced here: 70 us
  Pallas kernels  65.5 us (93%)
  local copies, waits for them, and re-layouts  4.48 us (6%)
    pallas_call x1, Pallas kernels, shards(): pl.pallas_call(functools.partial(kernel, n, sections), out_shape=jax.Shap...  65.5 us
    unnamed x1, local copies, waits for them, and re-layouts  1.72 us

profile of v1, /device:TPU:0, one launch (start us, length us, event | category | flops | bytes accessed | tf_op | source)
XLA Modules:
  0.0 70.0 jit_solution(7719763137985185220)
XLA Ops:
  0.0 1.4 %copy.14 = s32[2,1,32,2]{3,2,0,1:T(8,128)} copy(s32[2,1,32,2]{2,3,1,0:T(2,128)} %param.10) | data formatting | bytes 1024 | tf_op jit(solution)/shard_map/reshape | solution.py:399
  1.4 1.4 %copy.15 = f32[2,1,32,2]{3,2,0,1:T(8,128)} copy(f32[2,1,32,2]{2,3,1,0:T(2,128)} %param.11) | data formatting | bytes 1024 | tf_op jit(solution)/shard_map/reshape | solution.py:400
  2.8 65.5 %shard_map.82 = bf16[2,32,2560]{2,1,0:T(8,128)(2,1)} custom-call(bf16[32,2560]{1,0:T(8,128)(2,1)} %bitcast.13, bf16[1,32,2560]{2,1,0:T(8,128)(2,1)} %incoming.1, s32[64,2]{1,0:T(8,128)} %bitcast.14, f32[64,2]{1,0:T(8,128)} %bitcast.15, f32[1,2560]{1,0:T(1,128)} %gain.1, bf16[2560,768]{1,0:T(8,128)(2,1)} %bitcast.9, bf16[2560,768]{1,0:T(8,128)(2,1)} %bitcast.10, ...), custom_call_target="tpu_custom_call" | custom-call | tf_op jit(solution)/shard_map/pallas_call | solution.py:366
  68.2 1.7 %copy.19 = bf16[2,1,32,2560]{3,2,1,0:T(8,128)(2,1)} copy(bf16[2,1,32,2560]{3,2,1,0:T(8,128)(2,1)} %bitcast.12) | data formatting | bytes 655360

commit v2 on v1

--- a/solution.py
+++ b/solution.py
@@ -9,7 +9,8 @@
 
 MESH = pl.DeviceIdType.MESH
 EXPERTS = 4
-CHUNKS = 2
+CHUNKS = 4
+PIECES = 1
 RIGHT, LEFT = 0, 1
 
 
@@ -62,12 +63,19 @@
     has = (has_right, has_left)
     peer = (right, left)
 
-    weight_copies = [
-        pltpu.make_async_copy(src, dst, w_sem.at[i])
-        for i, (src, dst) in enumerate(
-            ((w_gate_hbm, w_gate), (w_up_hbm, w_up), (w_down_hbm, w_down))
-        )
-    ]
+    weight_copies = []
+    for i, (src, dst) in enumerate(
+        ((w_gate_hbm, w_gate), (w_up_hbm, w_up), (w_down_hbm, w_down))
+    ):
+        deep = src.shape[0] // PIECES
+        weight_copies.append(
+            [
+                pltpu.make_async_copy(
+                    src.at[pl.ds(p * deep, deep)], dst.at[pl.ds(p * deep, deep)], w_sem.at[i, p]
+                )
+                for p in range(PIECES)
+            ]
+        )
 
     def own_copy(c):
         return pltpu.make_async_copy(
@@ -135,8 +143,9 @@
         def _():
             pl.semaphore_signal(barrier, inc=1, device_id=device, device_id_type=MESH)
 
-    for copy in weight_copies:
-        copy.start()
+    for copies in weight_copies:
+        for copy in copies:
+            copy.start()
 
     @pl.when(jnp.logical_not(has_prev))
     def _():
@@ -144,19 +153,15 @@
             for c in range(chunks):
                 inc_copy(t, c).start()
 
-    rows = ticks * tokens
     lanes = mixbuf.shape[2]
-    eye = lax.broadcasted_iota(jnp.int32, (rows, lanes), 0) == lax.broadcasted_iota(
-        jnp.int32, (rows, lanes), 1
-    )
-    chosen = routes[...]
-    chosen_weight = route_weight[...]
     mixbuf[e] = jnp.zeros_like(mixbuf[e])
-    for x in range(EXPERTS):
-        column = jnp.sum(jnp.where(chosen == x, chosen_weight, 0.0), axis=1, keepdims=True)
-        mixbuf[e, x : x + 1, :] = jnp.sum(
-            jnp.where(eye, column, 0.0), axis=0, keepdims=True
-        )
+    for t in range(ticks):
+        chosen = routes[t, 0]
+        chosen_weight = route_weight[t, 0]
+        for x in range(EXPERTS):
+            mixbuf[e, t * EXPERTS + x : t * EXPERTS + x + 1, 0:tokens] = jnp.sum(
+                jnp.where(chosen == x, chosen_weight, 0.0), axis=0, keepdims=True
+            )
 
     pl.semaphore_wait(barrier, sum(jnp.where(there, 1, 0) for there, _ in around))
 
@@ -167,17 +172,29 @@
             def _():
                 ag_copy(way, t, e, c).start()
 
-    def partial_of(t, j):
-        squares = jnp.zeros((tokens, 1), jnp.float32)
-        for c in range(chunks):
-            piece = xbuf[t, j, c].astype(jnp.float32)
-            squares = squares + jnp.sum(piece * piece, axis=1, keepdims=True)
-        scale = lax.rsqrt(squares * (1.0 / width) + 1e-06)
+    def partial_of(t, blocks, first):
+        scales = []
+        for j in blocks:
+            squares = jnp.zeros((tokens, 1), jnp.float32)
+            for c in range(chunks):
+                piece = xbuf[t, j, c].astype(jnp.float32)
+                squares = squares + jnp.sum(piece * piece, axis=1, keepdims=True)
+            scales.append(lax.rsqrt(squares * (1.0 / width) + 1e-06))
+
+        @pl.when(first)
+        def _():
+            for copy in weight_copies[0] + weight_copies[1]:
+                copy.wait()
+
         gate_val = up_val = None
         for c in range(chunks):
             span = pl.ds(c * cols, cols)
-            normed = (xbuf[t, j, c].astype(jnp.float32) * scale * gain[:, span]).astype(
-                jnp.bfloat16
+            normed = jnp.concatenate(
+                [
+                    (xbuf[t, j, c].astype(jnp.float32) * scale * gain[:, span]).astype(jnp.bfloat16)
+                    for j, scale in zip(blocks, scales)
+                ],
+                axis=0,
             )
             gate_part = jnp.dot(normed, w_gate[span, :], preferred_element_type=jnp.float32)
             up_part = jnp.dot(normed, w_up[span, :], preferred_element_type=jnp.float32)
@@ -185,25 +202,40 @@
             up_val = up_part if up_val is None else up_val + up_part
         hidden = (jax.nn.silu(gate_val) * up_val).astype(jnp.bfloat16)
         expert = e // group
-        row = mixbuf[j, pl.ds(expert, 1), :]
-        pick = (
-            lax.broadcasted_iota(jnp.int32, (tokens, lanes), 0) + t * tokens
-            == lax.broadcasted_iota(jnp.int32, (tokens, lanes), 1)
-        )
-        mixing = jnp.sum(jnp.where(pick, row, 0.0), axis=1, keepdims=True)
+        pick = lax.broadcasted_iota(jnp.int32, (tokens, lanes), 0) == lax.broadcasted_iota(
+            jnp.int32, (tokens, lanes), 1
+        )
+        mixing = [
+            jnp.sum(
+                jnp.where(pick, mixbuf[j, pl.ds(t * EXPERTS + expert, 1), :], 0.0),
+                axis=1,
+                keepdims=True,
+            )
+            for j in blocks
+        ]
+
+        @pl.when(first)
+        def _():
+            for copy in weight_copies[2]:
+                copy.wait()
+
         for c in range(chunks):
             span = pl.ds(c * cols, cols)
-            value = jnp.dot(hidden, w_down[:, span], preferred_element_type=jnp.float32) * mixing
-            held[j, c] = value
-            for way, first in (
-                (RIGHT, jnp.logical_and(jnp.logical_not(has_left), j > e)),
-                (LEFT, jnp.logical_and(jnp.logical_not(has_right), j < e)),
-            ):
-
-                @pl.when(first)
-                def _():
-                    rsout[t, j, c] = value.astype(jnp.bfloat16)
-                    rs_copy(way, t, j, c).start()
+            values = jnp.dot(hidden, w_down[:, span], preferred_element_type=jnp.float32)
+            for i, j in enumerate(blocks):
+                value = values[i * tokens : (i + 1) * tokens] * mixing[i]
+                held[j, c] = value
+                if len(blocks) > 1:
+                    continue
+                for way, send in (
+                    (RIGHT, jnp.logical_and(jnp.logical_not(has_left), j > e)),
+                    (LEFT, jnp.logical_and(jnp.logical_not(has_right), j < e)),
+                ):
+
+                    @pl.when(send)
+                    def _():
+                        rsout[t, j, c] = value.astype(jnp.bfloat16)
+                        rs_copy(way, t, j, c).start()
 
     def tick(t, _):
         for c in range(chunks):
@@ -230,14 +262,11 @@
                 def _():
                     mix_copy(way, e).start()
 
-            for copy in weight_copies:
-                copy.wait()
-
-        def arrive(k, _):
+        def arrive(k):
             for c in range(chunks):
                 for way, j in ((RIGHT, e - k), (LEFT, e + k)):
 
-                    @pl.when(jnp.logical_and(k > 0, jnp.logical_and(j >= 0, j < n)))
+                    @pl.when(jnp.logical_and(j >= 0, j < n))
                     def _():
                         ag_copy(way, t, j, c).wait_recv()
 
@@ -255,22 +284,28 @@
                                 def _():
                                     mix_copy(way, j).start()
 
-            def side(way, _):
-                j = e + k * (2 * way - 1)
-
-                @pl.when(
-                    jnp.logical_and(
-                        jnp.logical_and(j >= 0, j < n), jnp.logical_or(k > 0, way == 0)
-                    )
-                )
-                def _():
-                    partial_of(t, j)
-
-                return 0
-
-            return lax.fori_loop(0, 2, side, 0)
-
-        lax.fori_loop(0, n, arrive, 0)
+        def step(i, _):
+            k = jnp.where(t == 0, lax.rem(i + 1, n), i)
+            there_left, there_right = e - k >= 0, e + k < n
+
+            @pl.when(k > 0)
+            def _():
+                arrive(k)
+
+            both = jnp.logical_and(k > 0, jnp.logical_and(there_left, there_right))
+            first = jnp.logical_and(t == 0, i == 0)
+
+            @pl.when(both)
+            def _():
+                partial_of(t, (e - k, e + k), first)
+
+            @pl.when(jnp.logical_and(jnp.logical_not(both), jnp.logical_or(there_left, there_right)))
+            def _():
+                partial_of(t, (jnp.where(there_left, e - k, e + k),), first)
+
+            return 0
+
+        lax.fori_loop(0, n, step, 0)
 
         from_right, from_left = 2 * (n - 1 - e), 2 * e
         last = jnp.maximum(from_right, from_left)
@@ -354,11 +389,12 @@
     sections = mesh.shape["section"]
 
     def shards(acts, incoming, routes, route_weight, norm_gain, w_gate, w_up, w_down):
-        ticks, _, tokens, top = routes.shape
+        ticks, _, tokens, _ = routes.shape
         width, hidden = w_gate.shape[1:]
         chunks = CHUNKS
         cols = width // chunks
-        lanes = -(-ticks * tokens // 128) * 128
+        lanes = -(-tokens // 128) * 128
+        table = -(-ticks * EXPERTS // 8) * 8
         half = jnp.bfloat16
         anywhere = pl.BlockSpec(memory_space=pl.ANY)
         vmem = pl.BlockSpec(memory_space=pltpu.VMEM)
@@ -373,12 +409,12 @@
                 pltpu.VMEM((width, hidden), half),
                 pltpu.VMEM((hidden, width), half),
                 pltpu.VMEM((ticks, n, chunks, tokens, cols), half),
-                pltpu.VMEM((n, 8, lanes), jnp.float32),
+                pltpu.VMEM((n, table, lanes), jnp.float32),
                 pltpu.VMEM((2, ticks, n, chunks, tokens, cols), half),
                 pltpu.VMEM((ticks, n, chunks, tokens, cols), half),
                 pltpu.VMEM((n, chunks, tokens, cols), jnp.float32),
                 pltpu.VMEM((ticks - 1, chunks, tokens, cols), half),
-                dma((3,)),
+                dma((3, PIECES)),
                 dma((chunks,)),
                 dma((ticks, chunks)),
                 dma((2, ticks, n, chunks)),
@@ -396,8 +432,8 @@
         )(
             acts[0],
             incoming,
-            routes.reshape(ticks * tokens, top),
-            route_weight.reshape(ticks * tokens, top),
+            jnp.swapaxes(routes, 2, 3),
+            jnp.swapaxes(route_weight, 2, 3),
             norm_gain,
             w_gate[0],
             w_up[0],

time: 70.2 us -> 64.9 us (0.925)
  local copies, waits for them, and re-layouts: 4.48 us -> 1.72 us
  Pallas kernels: 65.5 us -> 63 us
    reshape x2 -> x0, local copies, waits for them, and re-layouts: 2.76 us -> none  [the longest x1 1.38 us: shards(): routes.reshape(ticks * tokens, top)]
    pallas_call x1, Pallas kernels: 65.5 us -> 63 us  [shards(): pl.pallas_call(functools.partial(kernel, n, sections), out_shape=jax.Shap...]
where the time goes in v2:
time: 64.9 us; the launch traced here: 64.7 us
  Pallas kernels  63 us (97%)
  local copies, waits for them, and re-layouts  1.72 us (3%)
    pallas_call x1, Pallas kernels, shards(): pl.pallas_call(functools.partial(kernel, n, sections), out_shape=jax.Shap...  63 us
    unnamed x1, local copies, waits for them, and re-layouts  1.72 us

profile of v2, /device:TPU:0, one launch (start us, length us, event | category | flops | bytes accessed | tf_op | source)
XLA Modules:
  0.0 64.7 jit_solution(13759441306266922830)
XLA Ops:
  0.0 63.0 %shard_map.82 = bf16[2,32,2560]{2,1,0:T(8,128)(2,1)} custom-call(bf16[32,2560]{1,0:T(8,128)(2,1)} %bitcast.13, bf16[1,32,2560]{2,1,0:T(8,128)(2,1)} %incoming.1, s32[2,1,2,32]{3,2,1,0:T(2,128)} %bitcast.14, f32[2,1,2,32]{3,2,1,0:T(2,128)} %bitcast.15, f32[1,2560]{1,0:T(1,128)} %gain.1, bf16[2560,768]{1,0:T(8,128)(2,1)} %bitcast.9, ...), custom_call_target="tpu_custom_call" | custom-call | tf_op jit(solution)/shard_map/pallas_call | solution.py:402
  63.0 1.7 %copy.11 = bf16[2,1,32,2560]{3,2,1,0:T(8,128)(2,1)} copy(bf16[2,1,32,2560]{3,2,1,0:T(8,128)(2,1)} %bitcast.12) | data formatting | bytes 655360
